TPU v7x, 32 devices: a whole 2x2x4 slice. The times are simulated.
32 devices in a mesh: groups: 2 (over y), gcol: 8 (over z, x), grow: 2 (over core).
Axes of the slice: x: 2, y: 2, z: 4, core: 2. Of those that a mesh axis runs over, the one named last changes fastest.
Arguments:
- patches: bfloat16 [16, 256, 1024], P(('groups', 'grow'), 'gcol'), parts along dimension 0, may hold values from -6 to 6
- mask_token: bfloat16 [1024], replicated, may hold values from -6 to 6
- masked: int32 [16, 256], P(('groups', 'grow'), 'gcol'), parts along dimension 0, may hold values 0 or 1
- tissue: int32 [16, 256], P(('groups', 'grow'), 'gcol'), parts along dimension 0, may hold values 0 or 1
- in_weight: bfloat16 [2304, 1024], P(None, 'grow'), may hold values from -0.1875 to 0.1875
- out_weight: bfloat16 [1024, 1024], P(None, 'grow'), may hold values from -0.1875 to 0.1875
- row_decay: float32 [8, 16, 256], P(None, ('groups', 'grow'), 'gcol'), parts along dimension 1, may hold values from -1.5 to 0
- col_decay: float32 [8, 16, 256], P(None, ('groups', 'grow'), 'gcol'), parts along dimension 1, may hold values from -1.5 to 0
- cotangent: bfloat16 [16, 256, 1024], P(('groups', 'grow'), 'gcol'), parts along dimension 0, may hold values from -6 to 6
Outputs:
- patch_grad: bfloat16 [16, 256, 1024], P(('groups', 'grow'), 'gcol'), parts along dimension 0
- out_weight_grad: float32 [2048, 1024], P(('groups', 'gcol', 'grow')), parts along dimension 0
There are 2 independent parts, one for each index of `groups`. A program takes and returns all parts, laid end to end along the dimension named above; an argument that names none is the same for every part. Nothing has to cross between parts.
All inputs are finite; a program needn't handle non-finite values. No bound on the sum of `masked` or of `tissue` on one device may be relied on, other than what follows from the above.
Results may differ from a plain program's by a relative error of at most 0.0095.
The roundings to bfloat16 on the way count: a program that leaves them out, or rounds other values in their place, can miss the bound.
Values may be sent and summed in bfloat16 or wider, within the bound.
A program may use at most 320 MiB of HBM per device.

v0:
```python
import functools
import math

import jax
import jax.numpy as jnp
from jax import lax
from jax.experimental import pallas as pl
from jax.experimental.pallas import tpu as pltpu
from jax.sharding import PartitionSpec as P

E = 1024
HEADS = 16
N = 64


EPSILON = 1e-05
PRECISE = lax.Precision.HIGHEST


def prefix(value, axis, join, neutral):
    count, mine = (lax.axis_size(axis), lax.axis_index(axis))
    pieces = jax.tree.map(lambda part: lax.all_gather(part, axis), value)
    so_far = jax.tree.map(
        lambda part, zero: jnp.full_like(part, 0) + jnp.asarray(zero, part.dtype), value, neutral
    )

    def prefix_hop(position, so_far):
        longer = join(so_far, jax.tree.map(lambda part: part[position], pieces))
        return jax.tree.map(lambda new, old: jnp.where(position < mine, new, old), longer, so_far)

    return lax.fori_loop(0, count - 1, prefix_hop, so_far)


def carried_in(shard, axis, combine, identity):
    length, position = (lax.axis_size(axis), lax.axis_index(axis))
    everything = jax.tree.map(
        lambda part, kind: lax.all_gather(part.astype(kind), axis),
        shard,
        jax.tree.map(lambda a: jnp.bfloat16 if a.dtype == jnp.float32 else a.dtype, shard),
    )
    start = jax.tree.map(
        lambda part, zero: jnp.broadcast_to(jnp.asarray(zero, part.dtype), part.shape),
        shard,
        identity,
    )

    def carried_hop(k, before):
        at = length - 1 - k
        reached = at > position
        new = combine(
            before, jax.tree.map(lambda part, own: part[at].astype(own.dtype), everything, shard)
        )
        return jax.tree.map(lambda a, b: jnp.where(reached, a, b), new, before)

    return lax.fori_loop(0, length, carried_hop, start)


def shortened(shard):

    def short(part):
        return part.astype(jnp.bfloat16) if part.dtype == jnp.float32 else part

    return jax.tree.map(short, shard)


def silu_grad(pre_act):
    sigmoid_v = jax.nn.sigmoid(pre_act)
    return sigmoid_v * (1.0 + pre_act * (1.0 - sigmoid_v))


def per_channel(head_part, channels):
    return jnp.repeat(head_part, channels // head_part.shape[-1], axis=-1)


def line_form(head_lines, channels):
    return per_channel(head_lines.transpose(1, 2, 0), channels)


def carry_on(log_lines, state):
    return per_channel(jnp.exp(log_lines), state.shape[2])[:, None, :] * state


def prepare(log_decay):
    length = log_decay.shape[2]
    running = jnp.cumsum(log_decay, axis=2)
    whole_log = running[:, :, -1]
    causal = jnp.arange(length)[:, None] >= jnp.arange(length)[None, :]
    log_gaps = running[:, :, :, None] - running[:, :, None, :]
    decay_mat = jnp.where(causal, jnp.exp(jnp.where(causal, log_gaps, 0.0)), 0.0)
    return (running, whole_log, decay_mat)


def chain_link(earlier, later):
    return (earlier[0] + later[0], carry_on(later[0], earlier[1]) + later[1])


def split_heads(lines, head_count):
    line_count, length, channels = lines.shape
    return lines.reshape(line_count, length, head_count, channels // head_count)


def local_summary(inputs, key_vecs, prepared):
    running, whole_log, decay_mat = prepared
    to_end = line_form(jnp.exp(whole_log[:, :, None] - running), inputs.shape[2])
    fresh = jnp.einsum("ltc,ltn->lnc", inputs * to_end, key_vecs, precision=PRECISE)
    return (whole_log.T, fresh)


def local_return(query_vecs, prepared, upstream):
    running, whole_log, decay_mat = prepared
    from_start = line_form(jnp.exp(running), upstream.shape[2])
    backward = jnp.einsum("ltc,ltn->lnc", upstream * from_start, query_vecs, precision=PRECISE)
    return (whole_log.T, backward)


def local_outputs(inputs, key_vecs, query_vecs, prepared, incoming):
    running, whole_log, decay_mat = prepared
    head_count = decay_mat.shape[0]
    line_count, length, channels = inputs.shape
    scores = jnp.einsum("ltn,lkn->ltk", query_vecs, key_vecs, precision=PRECISE)
    within = jnp.einsum(
        "gltk,lkgp->ltgp",
        decay_mat * scores[None],
        split_heads(inputs, head_count),
        precision=PRECISE,
    )
    within = within.reshape(line_count, length, channels)
    carried = jnp.einsum("ltn,lnc->ltc", query_vecs, incoming, precision=PRECISE)
    return within + carried * line_form(jnp.exp(running), channels)


def local_grads(inputs, key_vecs, query_vecs, prepared, incoming, returning, upstream):
    running, whole_log, decay_mat = prepared
    head_count = decay_mat.shape[0]
    line_count, length, channels = inputs.shape
    from_start = line_form(jnp.exp(running), channels)
    to_end = line_form(jnp.exp(whole_log[:, :, None] - running), channels)
    scores = jnp.einsum("ltn,lkn->ltk", query_vecs, key_vecs, precision=PRECISE)
    heads_up = split_heads(upstream, head_count)
    heads_in = split_heads(inputs, head_count)
    grad_inputs = jnp.einsum(
        "gltk,ltgp->lkgp", decay_mat * scores[None], heads_up, precision=PRECISE
    ).reshape(line_count, length, channels)
    grad_inputs = (
        grad_inputs + jnp.einsum("lnc,lkn->lkc", returning, key_vecs, precision=PRECISE) * to_end
    )
    mixed = jnp.einsum("ltgp,lkgp->gltk", heads_up, heads_in, precision=PRECISE) * decay_mat
    grad_keys = jnp.einsum("gltk,ltn->lkn", mixed, query_vecs, precision=PRECISE)
    grad_keys = grad_keys + jnp.einsum(
        "lkc,lnc->lkn", inputs * to_end, returning, precision=PRECISE
    )
    grad_queries = jnp.einsum("gltk,lkn->ltn", mixed, key_vecs, precision=PRECISE)
    grad_queries = grad_queries + jnp.einsum(
        "ltc,lnc->ltn", upstream * from_start, incoming, precision=PRECISE
    )
    return (grad_inputs, grad_keys, grad_queries)


def shards(
    patches, mask_token, masked, tissue, in_weight, out_weight, row_decay, col_decay, cotangent
):
    grid_rows, grid_cols, feat_width = patches.shape
    tok_count = grid_rows * grid_cols
    chosen = (masked == 1)[:, :, None]
    present = tissue.astype(jnp.bfloat16)[:, :, None]
    model_in = jnp.where(chosen, mask_token[None, None, :], patches) * present
    flat_in = model_in.reshape(tok_count, feat_width)
    inner_width = E
    half_width = inner_width // 2
    state_size = N
    number_of_heads = HEADS // 2
    offset = 2 * inner_width
    full_in, full_out = (
        lax.all_gather(in_weight, "grow", axis=1, tiled=True),
        lax.all_gather(out_weight, "grow", axis=1, tiled=True),
    )
    projected = lax.dot_general(
        flat_in, full_in, (((1,), (1,)), ((), ())), preferred_element_type=jnp.float32
    )
    proj_bf = projected.astype(jnp.bfloat16)
    pre_values = proj_bf[:, :inner_width].astype(jnp.float32)
    gate_pre = proj_bf[:, inner_width:offset].astype(jnp.float32)
    key_rows = (
        proj_bf[:, offset : offset + state_size]
        .astype(jnp.float32)
        .reshape(grid_rows, grid_cols, state_size)
    )
    query_rows = (
        proj_bf[:, offset + state_size : offset + 2 * state_size]
        .astype(jnp.float32)
        .reshape(grid_rows, grid_cols, state_size)
    )
    key_cols = (
        proj_bf[:, offset + 2 * state_size : offset + 3 * state_size]
        .astype(jnp.float32)
        .reshape(grid_rows, grid_cols, state_size)
        .transpose(1, 0, 2)
    )
    query_cols = (
        proj_bf[:, offset + 3 * state_size : offset + 4 * state_size]
        .astype(jnp.float32)
        .reshape(grid_rows, grid_cols, state_size)
        .transpose(1, 0, 2)
    )
    values = jax.nn.silu(pre_values)
    row_inputs = values[:, :half_width].reshape(grid_rows, grid_cols, half_width)
    col_inputs = values[:, half_width:].reshape(grid_rows, grid_cols, half_width).transpose(1, 0, 2)
    row_prep = prepare(row_decay)
    col_prep = prepare(col_decay.transpose(0, 2, 1))
    row_zero = (
        jnp.zeros((grid_rows, number_of_heads), jnp.float32),
        jnp.zeros((grid_rows, state_size, half_width), jnp.float32),
    )
    col_zero = (
        jnp.zeros((grid_cols, number_of_heads), jnp.float32),
        jnp.zeros((grid_cols, state_size, half_width), jnp.float32),
    )
    row_entry = prefix(local_summary(row_inputs, key_rows, row_prep), "gcol", chain_link, row_zero)[
        1
    ]
    grow_size = lax.axis_size("grow")
    my_block = lax.axis_index("grow")
    parts_in, parts_key, parts_log = (
        lax.all_gather(
            proj_bf[:, half_width:inner_width].reshape(grid_rows, grid_cols, half_width),
            "grow",
            axis=0,
            tiled=True,
        ),
        lax.all_gather(
            proj_bf[:, offset + 2 * state_size : offset + 3 * state_size].reshape(
                grid_rows, grid_cols, state_size
            ),
            "grow",
            axis=0,
            tiled=True,
        ),
        lax.all_gather(
            col_decay.transpose(1, 0, 2).astype(jnp.bfloat16), "grow", axis=0, tiled=True
        ).astype(jnp.float32),
    )
    col_entry = col_zero[1]
    for block_idx in range(grow_size):
        lower_row = block_idx * grid_rows
        piece_in = jax.nn.silu(
            parts_in[lower_row : lower_row + grid_rows].astype(jnp.float32)
        ).transpose(1, 0, 2)
        piece_keys = (
            parts_key[lower_row : lower_row + grid_rows].astype(jnp.float32).transpose(1, 0, 2)
        )
        piece_log = parts_log[lower_row : lower_row + grid_rows].transpose(1, 2, 0)
        whole_log, piece_state = local_summary(piece_in, piece_keys, prepare(piece_log))
        moved = carry_on(whole_log, col_entry) + piece_state
        col_entry = jnp.where(block_idx < my_block, moved, col_entry)
    row_out = local_outputs(row_inputs, key_rows, query_rows, row_prep, row_entry)
    col_out = local_outputs(col_inputs, key_cols, query_cols, col_prep, col_entry).transpose(
        1, 0, 2
    )
    mixed = jnp.concatenate(
        [row_out.reshape(tok_count, half_width), col_out.reshape(tok_count, half_width)], axis=1
    )
    gate_act = jax.nn.silu(gate_pre)
    head_size = inner_width // HEADS
    gated = (mixed * gate_act).reshape(tok_count, HEADS, head_size)
    inv_rms = lax.rsqrt(jnp.mean(gated * gated, axis=2, keepdims=True) + EPSILON)
    normed = gated * inv_rms
    normed_bf = normed.reshape(tok_count, inner_width).astype(jnp.bfloat16)
    grad_out = (cotangent * masked.astype(jnp.bfloat16)[:, :, None]).reshape(tok_count, feat_width)
    total_patches = tok_count * lax.axis_size("gcol") * lax.axis_size("grow")
    weight_sum = lax.psum_scatter(
        lax.dot_general(
            grad_out, normed_bf, (((0,), (0,)), ((), ())), preferred_element_type=jnp.float32
        ),
        ("gcol", "grow"),
        scatter_dimension=0,
        tiled=True,
    )
    out_weight_grad = weight_sum * (1.0 / math.sqrt(total_patches))
    grad_normed_bf = jnp.dot(grad_out, full_out, preferred_element_type=jnp.float32).astype(
        jnp.bfloat16
    )
    grad_normed = lax.optimization_barrier(grad_normed_bf).astype(jnp.float32)
    grad_normed = grad_normed.reshape(tok_count, HEADS, head_size)
    grad_gated = inv_rms * (
        grad_normed - normed * jnp.mean(grad_normed * normed, axis=2, keepdims=True)
    )
    grad_gated = grad_gated.reshape(tok_count, inner_width)
    grad_mixed = grad_gated * gate_act
    grad_gate = grad_gated * mixed * silu_grad(gate_pre)
    row_up = grad_mixed[:, :half_width].reshape(grid_rows, grid_cols, half_width)
    col_up = grad_mixed[:, half_width:].reshape(grid_rows, grid_cols, half_width).transpose(1, 0, 2)
    row_exit = carried_in(local_return(query_rows, row_prep, row_up), "gcol", chain_link, row_zero)[
        1
    ]
    parts_up, parts_query = (
        lax.all_gather(
            shortened(grad_mixed[:, half_width:].reshape(grid_rows, grid_cols, half_width)),
            "grow",
            axis=0,
            tiled=True,
        ),
        lax.all_gather(
            proj_bf[:, offset + 3 * state_size : offset + 4 * state_size].reshape(
                grid_rows, grid_cols, state_size
            ),
            "grow",
            axis=0,
            tiled=True,
        ),
    )
    col_exit = col_zero[1]
    for block_idx in reversed(range(grow_size)):
        lower_row = block_idx * grid_rows
        piece_up = parts_up[lower_row : lower_row + grid_rows].transpose(1, 0, 2)
        piece_queries = (
            parts_query[lower_row : lower_row + grid_rows].astype(jnp.float32).transpose(1, 0, 2)
        )
        piece_log = parts_log[lower_row : lower_row + grid_rows].transpose(1, 2, 0)
        whole_log, piece_back = local_return(piece_queries, prepare(piece_log), piece_up)
        moved = carry_on(whole_log, col_exit) + piece_back
        col_exit = jnp.where(block_idx > my_block, moved, col_exit)
    grad_row_in, grad_row_key, grad_row_query = local_grads(
        row_inputs, key_rows, query_rows, row_prep, row_entry, row_exit, row_up
    )
    grad_col_in, grad_col_key, grad_col_query = local_grads(
        col_inputs, key_cols, query_cols, col_prep, col_entry, col_exit, col_up
    )
    grad_values = jnp.concatenate(
        [
            grad_row_in.reshape(tok_count, half_width),
            grad_col_in.transpose(1, 0, 2).reshape(tok_count, half_width),
        ],
        axis=1,
    )
    grad_proj = jnp.concatenate(
        [
            grad_values * silu_grad(pre_values),
            grad_gate,
            grad_row_key.reshape(tok_count, state_size),
            grad_row_query.reshape(tok_count, state_size),
            grad_col_key.transpose(1, 0, 2).reshape(tok_count, state_size),
            grad_col_query.transpose(1, 0, 2).reshape(tok_count, state_size),
        ],
        axis=1,
    ).astype(jnp.bfloat16)
    keep_mask = present * (1 - masked).astype(jnp.bfloat16)[:, :, None]
    grad_model_in = jnp.dot(grad_proj, full_in, preferred_element_type=jnp.float32).reshape(
        grid_rows, grid_cols, feat_width
    )
    patch_grad = (grad_model_in * keep_mask).astype(jnp.bfloat16)
    return (patch_grad, out_weight_grad)


MESH = pl.DeviceIdType.MESH
NT = (((1,), (1,)), ((), ()))
NN = (((1,), (0,)), ((), ()))
TN = (((0,), (0,)), ((), ()))


def mm(a, b, dims):
    return lax.dot_general(a, b, dims, preferred_element_type=jnp.float32)


def layer_kernel(
    chips, rows, scale,
    patch_ref, token_ref, cot_ref, flag_ref, rdec_ref, cdec_ref, w_hbm, wout_hbm,
    pg_ref, out_ref,
    xs, gs, rd, cd, xb, gb, db, wa, wb, wout, u_s, z_s, gn_s, bc_s, normed_s, y_s, mat_s, dec_s, gp, grow, gcol,
    xsend, wgo, xr, zs, zr,
    x_send, x_recv, g_send, g_recv, d_send, d_recv, w_sem, l_sem,
    gp_send, gp_recv, xr_send, xr_recv, z_send, z_recv,
):
    k, c = lax.axis_index("gcol"), lax.axis_index("grow")
    depth = chips // 2
    zi, xi = k // 2, lax.rem(k, 2)
    cols, feat = patch_ref.shape[1], patch_ref.shape[2]
    toks = chips * cols
    half, part = wout.shape[1], wa.shape[1]
    total = 2 * chips

    load_w = pltpu.make_async_copy(w_hbm, wa, l_sem.at[0])
    load_o = pltpu.make_async_copy(wout_hbm, wout, l_sem.at[1])
    load_w.start()
    load_o.start()

    me = 2 * k + c
    barrier = pltpu.get_barrier_semaphore()
    for d in range(1, total):
        to = lax.rem(me + d, total)
        pl.semaphore_signal(
            barrier, inc=1, device_id={"gcol": to // 2, "grow": lax.rem(to, 2)}, device_id_type=MESH
        )

    def remote(src, dst, s, r, chip, core):
        return pltpu.make_async_remote_copy(
            src_ref=src, dst_ref=dst, send_sem=s, recv_sem=r,
            device_id={"gcol": chip, "grow": core}, device_id_type=MESH,
        )

    for i in range(rows):
        flags = flag_ref[i]
        hidden, present = flags[:, 0:1], flags[:, 1:2]
        chosen = jnp.where(
            hidden > 0.5, token_ref[...].astype(jnp.float32), patch_ref[i].astype(jnp.float32)
        )
        xs[i] = (chosen * present).astype(jnp.bfloat16)
        gs[i] = (cot_ref[i].astype(jnp.float32) * hidden).astype(jnp.bfloat16)
        rd[i] = rdec_ref[:, i, :]
        cd[i] = cdec_ref[:, i, :]

    streams = (
        (xs, xs, xb, x_send, x_recv),
        (rd, cd, db, d_send, d_recv),
        (gs, gs, gb, g_send, g_recv),
    )

    def row_out(stream, i):
        row_src, _, dst, s, r = stream
        return remote(row_src.at[i], dst.at[k], s.at[i], r.at[k], rows * c + i, 0)

    def col_out(stream):
        _, col_src, dst, s, r = stream
        return remote(col_src, dst.at[pl.ds(0, rows)], s.at[rows], r.at[chips], k, 1)

    def row_in(stream, src):
        row_src, _, dst, s, r = stream
        return remote(row_src.at[0], dst.at[src], s.at[0], r.at[src], k, 1 - c)

    def col_in(stream):
        _, col_src, dst, s, r = stream
        return remote(col_src, dst.at[pl.ds(0, rows)], s.at[rows], r.at[chips], k, 1 - c)

    def launch(stream):
        for i in range(rows):

            @pl.when(jnp.logical_or(c == 1, k != i))
            def _():
                row_out(stream, i).start()

        @pl.when(c == 0)
        def _():
            col_out(stream).start()

    def arrive(stream):
        @pl.when(c == 0)
        def _():
            for d in range(1, chips):
                row_in(stream, lax.rem(k + d, chips)).wait_recv()

            @pl.when(k >= rows)
            def _():
                row_in(stream, k).wait_recv()

        @pl.when(c == 1)
        def _():
            col_in(stream).wait_recv()

    def drain(stream):
        for i in range(rows):

            @pl.when(jnp.logical_or(c == 1, k != i))
            def _():
                row_out(stream, i).wait_send()

        @pl.when(c == 0)
        def _():
            col_out(stream).wait_send()

    pl.semaphore_wait(barrier, total - 1)
    weights = remote(w_hbm, wb, w_sem.at[0], w_sem.at[1], k, 1 - c)
    launch(streams[0])
    launch(streams[1])
    weights.start()
    launch(streams[2])

    for row_src, col_src, dst, _, _ in streams:

        @pl.when(c == 1)
        def _():
            dst[pl.ds(rows, rows)] = col_src[...]

        for i in range(rows):

            @pl.when(jnp.logical_and(c == 0, k == i))
            def _():
                dst[i] = row_src[i]

    t_at = lax.broadcasted_iota(jnp.int32, (toks, toks), 0)
    k_at = lax.broadcasted_iota(jnp.int32, (toks, toks), 1)
    step = jnp.where(c == 0, 1, cols)
    mask = jnp.logical_and(t_at >= k_at, lax.rem(t_at, step) == lax.rem(k_at, step))
    low = lax.broadcasted_iota(jnp.int32, (toks, 128), 1) < N

    arrive(streams[1])
    ones = mask.astype(jnp.float32)
    dec = jnp.concatenate([db[i] for i in range(chips)], axis=1)
    run_s = lax.dot_general(ones, dec, NT, precision=PRECISE, preferred_element_type=jnp.float32)
    run_l = lax.dot_general(dec, ones, NT, precision=PRECISE, preferred_element_type=jnp.float32)
    heads = dec.shape[0]
    for h in range(heads):
        gap = run_s[:, h : h + 1] - run_l[h : h + 1, :]
        dec_s[h] = jnp.where(mask, jnp.exp(jnp.minimum(gap, 0.0)), 0.0)

    load_w.wait()
    arrive(streams[0])
    mine, rest = pl.multiple_of(c * part, part), pl.multiple_of((1 - c) * part, part)
    own = xb[:, :, pl.ds(mine, part)].reshape(toks, part)
    oth = xb[:, :, pl.ds(rest, part)].reshape(toks, part)
    pieces = ((u_s, c * half, half), (z_s, 2 * half + c * half, half), (bc_s, 4 * half + c * 2 * N, 2 * N))
    partial = [
        mm(own, wa[pl.ds(pl.multiple_of(start, 128), size), :], NT) for _, start, size in pieces
    ]
    weights.wait_recv()
    for (dst, start, size), first in zip(pieces, partial):
        second = mm(oth, wb[pl.ds(pl.multiple_of(start, 128), size), :], NT)
        dst[...] = (first + second).astype(jnp.bfloat16)

    b_bf, c_bf = bc_s[:, :N], bc_s[:, N:]
    scores = mm(c_bf, b_bf, NT)

    def per_head(x):
        first = jnp.sum(jnp.where(low, x, 0.0), axis=1, keepdims=True)
        second = jnp.sum(jnp.where(low, 0.0, x), axis=1, keepdims=True)
        return jnp.where(low, first, second) * (1.0 / N)

    def norm(p):
        cols_p = slice(p * 128, (p + 1) * 128)
        z = z_s[:, cols_p].astype(jnp.float32)
        sig_z = 1.0 / (1.0 + jnp.exp(-z))
        y = y_s[:, cols_p]
        gated = y * (z * sig_z)
        inv = lax.rsqrt(per_head(gated * gated) + EPSILON)
        return cols_p, z, sig_z, y, inv, gated * inv

    for p in range(half // 128):
        cols_p = slice(p * 128, (p + 1) * 128)
        u = u_s[:, cols_p].astype(jnp.float32)
        val_bf = (u / (1.0 + jnp.exp(-u))).astype(jnp.bfloat16)
        for h in (2 * p, 2 * p + 1):
            mat_s[h] = (dec_s[h] * scores).astype(jnp.bfloat16)
        y_s[:, cols_p] = jnp.where(
            low, mm(mat_s[2 * p], val_bf, NN), mm(mat_s[2 * p + 1], val_bf, NN)
        )
        normed_s[:, cols_p] = norm(p)[-1].astype(jnp.bfloat16)

    load_o.wait()
    arrive(streams[2])

    def weight_block(chip):
        at = pl.ds(pl.multiple_of(chip * 128, 128), 128)
        return mm(gb[:, :, at].reshape(toks, 128), normed_s[...], TN)

    def across(q):
        return remote(xsend.at[q], xr.at[q], xr_send.at[q], xr_recv.at[q], 2 * zi + 1 - xi, c)

    order = [lax.rem(zi + 1 + j, depth) for j in range(depth)]
    for q in order:
        xsend[q] = weight_block(2 * q + 1 - xi).astype(jnp.bfloat16)
        across(q).start()

    grads = gb[...].reshape(toks, feat)
    gn_s[...] = mm(grads, wout[...], NN).astype(jnp.bfloat16)
    d_scores = jnp.zeros((toks, toks), jnp.float32)
    for p in range(half // 128):
        cols_p, z, sig_z, y, inv, normed = norm(p)
        u = u_s[:, cols_p].astype(jnp.float32)
        sig_u = 1.0 / (1.0 + jnp.exp(-u))
        val_bf = (u * sig_u).astype(jnp.bfloat16)
        gn = gn_s[:, cols_p].astype(jnp.float32)
        gg = inv * (gn - normed * per_head(gn * normed))
        dy = gg * (z * sig_z)
        dz = gg * y * (sig_z * (1.0 + z * (1.0 - sig_z)))
        dy_bf = dy.astype(jnp.bfloat16)
        dv = jnp.where(low, mm(mat_s[2 * p], dy_bf, TN), mm(mat_s[2 * p + 1], dy_bf, TN))
        du = dv * (sig_u * (1.0 + u * (1.0 - sig_u)))
        gp[:, :, cols_p] = du.astype(jnp.bfloat16).reshape(chips, cols, 128)
        gp[:, :, half + p * 128 : half + (p + 1) * 128] = dz.astype(jnp.bfloat16).reshape(
            chips, cols, 128
        )
        zero = jnp.zeros_like(dy)
        d_scores += dec_s[2 * p] * mm(jnp.where(low, dy, zero).astype(jnp.bfloat16), val_bf, NT)
        d_scores += dec_s[2 * p + 1] * mm(jnp.where(low, zero, dy).astype(jnp.bfloat16), val_bf, NT)
    ds_bf = d_scores.astype(jnp.bfloat16)
    d_bc = jnp.concatenate([mm(ds_bf, c_bf, TN), mm(ds_bf, b_bf, NN)], axis=1)
    gp[:, :, 2 * half :] = d_bc.astype(jnp.bfloat16).reshape(chips, cols, 2 * N)

    home, slot = k // rows, lax.rem(k, rows)

    def row_back(chip):
        return remote(gp.at[chip], grow.at[slot], gp_send.at[chip], gp_recv.at[slot], chip, home)

    def col_back(core):
        lo = pl.ds(0, rows)
        return remote(gp.at[lo], gcol, gp_send.at[chips], gp_recv.at[rows], k, core)

    @pl.when(c == 0)
    def _():
        for d in range(1, chips):
            row_back(lax.rem(k + d, chips)).start()

        @pl.when(home == 1)
        def _():
            row_back(k).start()

        for i in range(rows):

            @pl.when(k == i)
            def _():
                grow[i] = gp[i]

    @pl.when(c == 1)
    def _():
        col_back(0).start()
        gcol[...] = gp[pl.ds(rows, rows)]

    for q in range(depth):
        wgo[q] = weight_block(2 * q + xi)

    def along(q, core):
        return remote(
            zs.at[q, core], zr.at[zi, c], z_send.at[2 * q + core], z_recv.at[2 * zi + c], 2 * q + xi, core
        )

    def forward(q):
        across(q).wait_recv()
        both = wgo[q] + xr[q].astype(jnp.float32)
        wgo[q] = both
        zs[q] = both.astype(jnp.bfloat16).reshape(2, both.shape[0] // 2, both.shape[1])

    def forward_far(q):
        forward(q)
        for core in range(2):
            along(q, core).start()

    def back_project(src, g, w_ref):
        flat = src[...].reshape(rows * cols, 2 * half + 2 * N)
        acc = mm(flat[:, :half], w_ref[g * half : (g + 1) * half, :], NN)
        acc += mm(flat[:, half : 2 * half], w_ref[(2 + g) * half : (3 + g) * half, :], NN)
        at = 4 * half + g * 2 * N
        return acc + mm(flat[:, 2 * half :], w_ref[at : at + 2 * N, :], NN)

    forward_far(order[0])

    @pl.when(c == 0)
    def _():
        col_back(1).wait_recv()

    col_part = [back_project(gcol, 1, w_ref) for w_ref in (wa, wb)]
    for q in order[1:-1]:
        forward_far(q)
    forward(zi)
    along(zi, 1 - c).start()

    for i in range(rows):

        @pl.when(jnp.logical_or(c == 1, k != i))
        def _():
            remote(gp.at[0], grow.at[i], gp_send.at[0], gp_recv.at[i], k, 1 - c).wait_recv()

    for w_ref, at, first in ((wa, mine, col_part[0]), (wb, rest, col_part[1])):
        acc = (first + back_project(grow, 0, w_ref)).reshape(rows, cols, part)
        for i in range(rows):
            flags = flag_ref[i]
            keep = flags[:, 1:2] * (1.0 - flags[:, 0:1])
            pg_ref[i, :, pl.ds(at, part)] = (acc[i] * keep).astype(pg_ref.dtype)

    for q in order[:-1]:
        for core in range(2):
            remote(zs.at[0, 0], zr.at[q, core], z_send.at[0], z_recv.at[2 * q + core], k, 1 - c).wait_recv()
    remote(zs.at[0, 0], zr.at[zi, 1 - c], z_send.at[0], z_recv.at[2 * zi + 1 - c], k, 1 - c).wait_recv()
    zr[zi, c] = zs[zi, c]
    for core in range(2):
        acc = zr[0, core].astype(jnp.float32)
        for q in range(1, depth):
            acc += zr[q, core].astype(jnp.float32)
        out_ref[:, core * half : (core + 1) * half] = acc * scale

    for stream in streams:
        drain(stream)
    weights.wait_send()
    for q in order:
        across(q).wait_send()
    for q in order[:-1]:
        for core in range(2):
            along(q, core).wait_send()
    along(zi, 1 - c).wait_send()

    @pl.when(c == 0)
    def _():
        for d in range(1, chips):
            row_back(lax.rem(k + d, chips)).wait_send()

        @pl.when(home == 1)
        def _():
            row_back(k).wait_send()

    @pl.when(c == 1)
    def _():
        col_back(0).wait_send()


def owned(
    patches, mask_token, masked, tissue, in_weight, out_weight, row_decay, col_decay, cotangent
):
    rows, cols, feat = patches.shape
    chips = lax.axis_size("gcol")
    toks, heads = chips * cols, row_decay.shape[0]
    half, part = out_weight.shape[1], in_weight.shape[1]
    width = 2 * half + 2 * N
    slab = feat // (2 * chips)
    depth = chips // 2
    flags = jnp.stack([masked, tissue], axis=2).astype(jnp.float32)
    bf, fl = jnp.bfloat16, jnp.float32
    vmem, dma = pltpu.VMEM, pltpu.SemaphoreType.DMA
    in_vmem, anywhere = pl.BlockSpec(memory_space=pltpu.VMEM), pl.BlockSpec(memory_space=pl.ANY)
    scale = 1.0 / math.sqrt(2 * rows * cols * chips)
    return pl.pallas_call(
        functools.partial(layer_kernel, chips, rows, scale),
        name="layer",
        out_shape=(
            jax.ShapeDtypeStruct(patches.shape, bf),
            jax.ShapeDtypeStruct((slab, 2 * half), fl),
        ),
        in_specs=[in_vmem] * 6 + [anywhere] * 2,
        out_specs=(in_vmem, in_vmem),
        scratch_shapes=[
            vmem((rows, cols, feat), bf), vmem((rows, cols, feat), bf),
            vmem((rows, heads, cols), fl), vmem((rows, heads, cols), fl),
            vmem((chips, cols, feat), bf), vmem((chips, cols, feat), bf), vmem((chips, heads, cols), fl),
            vmem(in_weight.shape, bf), vmem(in_weight.shape, bf), vmem(out_weight.shape, bf),
            vmem((toks, half), bf), vmem((toks, half), bf), vmem((toks, half), bf),
            vmem((toks, 2 * N), bf), vmem((toks, half), bf), vmem((toks, half), fl),
            vmem((heads, toks, toks), bf), vmem((heads, toks, toks), fl),
            vmem((chips, cols, width), bf), vmem((rows, cols, width), bf), vmem((rows, cols, width), bf),
            vmem((depth, 2 * slab, half), bf), vmem((depth, 2 * slab, half), fl),
            vmem((depth, 2 * slab, half), bf), vmem((depth, 2, slab, half), bf),
            vmem((depth, 2, slab, half), bf),
            dma((rows + 1,)), dma((chips + 1,)), dma((rows + 1,)), dma((chips + 1,)),
            dma((rows + 1,)), dma((chips + 1,)), dma((2,)), dma((2,)),
            dma((chips + 1,)), dma((rows + 1,)), dma((depth,)), dma((depth,)),
            dma((2 * depth,)), dma((2 * depth,)),
        ],
        compiler_params=pltpu.CompilerParams(
            collective_id=0, has_side_effects=True, vmem_limit_bytes=48 << 20
        ),
    )(
        patches, mask_token.reshape(1, feat), cotangent, flags, row_decay, col_decay,
        in_weight, out_weight,
    )


def body(*args):
    rows = args[0].shape[0]
    if lax.axis_size("grow") == 2 and lax.axis_size("gcol") == 2 * rows:
        return owned(*args)
    return shards(*args)


def solution(mesh):
    return jax.shard_map(
        body,
        mesh=mesh,
        in_specs=(
            P(("groups", "grow"), "gcol", None),
            P(),
            P(("groups", "grow"), "gcol"),
            P(("groups", "grow"), "gcol"),
            P(None, "grow"),
            P(None, "grow"),
            P(None, ("groups", "grow"), "gcol"),
            P(None, ("groups", "grow"), "gcol"),
            P(("groups", "grow"), "gcol", None),
        ),
        out_specs=(P(("groups", "grow"), "gcol", None), P(("groups", "gcol", "grow"), None)),
        check_vma=False,
    )
```

profile of v0, /device:TPU:27, one launch (start us, length us, event | category | flops | bytes accessed | tf_op | source)
XLA Modules:
  0.0 49.7 jit_solution(1152777672583275149)
XLA Ops:
  0.6 0.7 %reshape.7.token_ref = bf16[1,1024]{1,0:T(2,128)(2,1)S(1)} reshape(bf16[1024]{0:T(1024)(128)(2,1)} %param.10) | data formatting | bytes 4096 | tf_op jit(solution)/shard_map/reshape | solution.py:747
  1.3 0.7 %add_convert_fusion = f32[4,32,2]{1,0,2:T(4,128)S(1)} fusion(s32[4,32,1]{1,0,2:T(4,128)} %bitcast.2, s32[4,32,1]{1,0,2:T(4,128)} %bitcast.3), kind=kLoop, calls=%fused_computation | loop fusion | flops 512 | bytes 2048 | tf_op jit(solution)/shard_map/convert_element_type | solution.py:712
  2.0 0.1 copy.14.flag_ref
  2.1 0.0 copy-start
  2.1 1.7 %copy-done = bf16[2304,512]{1,0:T(8,128)(2,1)S(1)} copy-done((bf16[2304,512]{1,0:T(8,128)(2,1)S(1)}, bf16[2304,512]{1,0:T(8,128)(2,1)}, u32[]{:S(2)}) %copy-start) | copy-done | bytes 2359320
  3.8 0.0 copy-start.1
  3.8 1.2 %copy-done.1 = bf16[1024,512]{1,0:T(8,128)(2,1)S(1)} copy-done((bf16[1024,512]{1,0:T(8,128)(2,1)S(1)}, bf16[1024,512]{1,0:T(8,128)(2,1)}, u32[]{:S(2)}) %copy-start.1) | copy-done | bytes 1048600
  5.0 0.0 copy-start.2
  5.0 0.9 %copy-done.2 = bf16[4,32,1024]{2,1,0:T(8,128)(2,1)S(1)} copy-done((bf16[4,32,1024]{2,1,0:T(8,128)(2,1)S(1)}, bf16[4,32,1024]{2,1,0:T(8,128)(2,1)}, u32[]{:S(2)}) %copy-start.2) | copy-done | bytes 262168
  6.0 0.0 copy-start.3
  6.0 0.9 %copy-done.3 = bf16[4,32,1024]{2,1,0:T(8,128)(2,1)S(1)} copy-done((bf16[4,32,1024]{2,1,0:T(8,128)(2,1)S(1)}, bf16[4,32,1024]{2,1,0:T(8,128)(2,1)}, u32[]{:S(2)}) %copy-start.3) | copy-done | bytes 262168
  6.9 0.0 copy-start.4
  6.9 0.7 %copy-done.4 = f32[8,4,32]{2,1,0:T(4,128)S(1)} copy-done((f32[8,4,32]{2,1,0:T(4,128)S(1)}, f32[8,4,32]{2,1,0:T(4,128)}, u32[]{:S(2)}) %copy-start.4) | copy-done | bytes 4120
  7.6 0.0 copy-start.5
  7.6 0.7 %copy-done.5 = f32[8,4,32]{2,1,0:T(4,128)S(1)} copy-done((f32[8,4,32]{2,1,0:T(4,128)S(1)}, f32[8,4,32]{2,1,0:T(4,128)}, u32[]{:S(2)}) %copy-start.5) | copy-done | bytes 4120
  8.4 39.9 %layer.1 = (bf16[4,32,1024]{2,1,0:T(8,128)(2,1)S(1)}, f32[64,1024]{1,0:T(8,128)S(1)}) custom-call(bf16[4,32,1024]{2,1,0:T(8,128)(2,1)S(1)} %copy-done.2, bf16[1,1024]{1,0:T(2,128)(2,1)S(1)} %reshape.7.token_ref, bf16[4,32,1024]{2,1,0:T(8,128)(2,1)S(1)} %copy-done.3, f32[4,32,2]{2,1,0:T(8,128)S(1)} %copy.14.flag_ref, f32[8,4,32]{2,1,0:T(4,128)S(1)} %copy-done.4, ...), custom_call_target="tpu_custom_call" | custom-call | tf_op jit(solution)/shard_map/layer/pallas_call | solution.py:717
  48.2 0.7 %copy.17 = bf16[4,32,1024]{2,1,0:T(8,128)(2,1)} copy(bf16[4,32,1024]{2,1,0:T(8,128)(2,1)S(1)} %get-tuple-element.4) | data formatting | bytes 524288
  48.9 0.7 %copy.18 = f32[64,1024]{1,0:T(8,128)} copy(f32[64,1024]{1,0:T(8,128)S(1)} %get-tuple-element.5) | data formatting | bytes 524288
Async XLA Ops:
  2.1 1.7 %copy-start = (bf16[2304,512]{1,0:T(8,128)(2,1)S(1)}, bf16[2304,512]{1,0:T(8,128)(2,1)}, u32[]{:S(2)}) copy-start(bf16[2304,512]{1,0:T(8,128)(2,1)} %w_hbm.1) | copy-start | bytes 7077892
  3.8 1.2 %copy-start.1 = (bf16[1024,512]{1,0:T(8,128)(2,1)S(1)}, bf16[1024,512]{1,0:T(8,128)(2,1)}, u32[]{:S(2)}) copy-start(bf16[1024,512]{1,0:T(8,128)(2,1)} %wout_hbm.1) | copy-start | bytes 3145732
  5.0 0.9 %copy-start.2 = (bf16[4,32,1024]{2,1,0:T(8,128)(2,1)S(1)}, bf16[4,32,1024]{2,1,0:T(8,128)(2,1)}, u32[]{:S(2)}) copy-start(bf16[4,32,1024]{2,1,0:T(8,128)(2,1)} %patch_ref.1) | copy-start | bytes 786436
  6.0 0.9 %copy-start.3 = (bf16[4,32,1024]{2,1,0:T(8,128)(2,1)S(1)}, bf16[4,32,1024]{2,1,0:T(8,128)(2,1)}, u32[]{:S(2)}) copy-start(bf16[4,32,1024]{2,1,0:T(8,128)(2,1)} %cot_ref.1) | copy-start | bytes 786436
  6.9 0.7 %copy-start.4 = (f32[8,4,32]{2,1,0:T(4,128)S(1)}, f32[8,4,32]{2,1,0:T(4,128)}, u32[]{:S(2)}) copy-start(f32[8,4,32]{2,1,0:T(4,128)} %rdec_ref.1) | copy-start | bytes 12292
  7.6 0.7 %copy-start.5 = (f32[8,4,32]{2,1,0:T(4,128)S(1)}, f32[8,4,32]{2,1,0:T(4,128)}, u32[]{:S(2)}) copy-start(f32[8,4,32]{2,1,0:T(4,128)} %cdec_ref.1) | copy-start | bytes 12292
where the time goes:
time: 50.1 us; the launch traced here: 49.7 us
  Pallas kernels  39.9 us (80%)
  local copies, waits for them, and re-layouts  8.42 us (17%)
  other arithmetic  0.7 us (1%)
  between operations  0.65 us (1%)
    pallas_call x1, Pallas kernels, owned(): pl.pallas_call(functools.partial(layer_kernel, chips, rows, scale), name=...  39.9 us
    unnamed x14, local copies, waits for them, and re-layouts  7.63 us

commit v1 on v0

--- a/solution.py
+++ b/solution.py
@@ -363,8 +363,9 @@
 
 def layer_kernel(
     chips, rows, scale,
-    patch_ref, token_ref, cot_ref, flag_ref, rdec_ref, cdec_ref, w_hbm, wout_hbm,
+    patch_hbm, token_hbm, cot_hbm, hidden_hbm, present_hbm, rdec_hbm, cdec_hbm, w_hbm, wout_hbm,
     pg_ref, out_ref,
+    patch_ref, token_ref, cot_ref, hidden_ref, present_ref, rdec_ref, cdec_ref, in_sem,
     xs, gs, rd, cd, xb, gb, db, wa, wb, wout, u_s, z_s, gn_s, bc_s, normed_s, y_s, mat_s, dec_s, gp, grow, gcol,
     xsend, wgo, xr, zs, zr,
     x_send, x_recv, g_send, g_recv, d_send, d_recv, w_sem, l_sem,
@@ -373,13 +374,24 @@
     k, c = lax.axis_index("gcol"), lax.axis_index("grow")
     depth = chips // 2
     zi, xi = k // 2, lax.rem(k, 2)
-    cols, feat = patch_ref.shape[1], patch_ref.shape[2]
+    cols, feat = xs.shape[1], xs.shape[2]
     toks = chips * cols
     half, part = wout.shape[1], wa.shape[1]
     total = 2 * chips
 
     load_w = pltpu.make_async_copy(w_hbm, wa, l_sem.at[0])
     load_o = pltpu.make_async_copy(wout_hbm, wout, l_sem.at[1])
+    loads = [
+        pltpu.make_async_copy(src, dst, in_sem.at[i])
+        for i, (src, dst) in enumerate(
+            (
+                (hidden_hbm, hidden_ref), (present_hbm, present_ref), (token_hbm, token_ref),
+                (patch_hbm, patch_ref), (rdec_hbm, rdec_ref), (cdec_hbm, cdec_ref), (cot_hbm, cot_ref),
+            )
+        )
+    ]
+    for copy in loads:
+        copy.start()
     load_w.start()
     load_o.start()
 
@@ -397,14 +409,18 @@
             device_id={"gcol": chip, "grow": core}, device_id_type=MESH,
         )
 
+    for copy in loads[:-1]:
+        copy.wait()
+    square = (cols, cols)
+    eye = lax.broadcasted_iota(jnp.int32, square, 0) == lax.broadcasted_iota(jnp.int32, square, 1)
+    eye = eye.astype(jnp.float32)
+    hidden_t = mm(eye, hidden_ref[...].astype(jnp.float32), NT)
+    present_t = mm(eye, present_ref[...].astype(jnp.float32), NT)
+    token = token_ref[...].reshape(1, feat).astype(jnp.float32)
     for i in range(rows):
-        flags = flag_ref[i]
-        hidden, present = flags[:, 0:1], flags[:, 1:2]
-        chosen = jnp.where(
-            hidden > 0.5, token_ref[...].astype(jnp.float32), patch_ref[i].astype(jnp.float32)
-        )
+        hidden, present = hidden_t[:, i : i + 1], present_t[:, i : i + 1]
+        chosen = jnp.where(hidden > 0.5, token, patch_ref[i].astype(jnp.float32))
         xs[i] = (chosen * present).astype(jnp.bfloat16)
-        gs[i] = (cot_ref[i].astype(jnp.float32) * hidden).astype(jnp.bfloat16)
         rd[i] = rdec_ref[:, i, :]
         cd[i] = cdec_ref[:, i, :]
 
@@ -471,6 +487,9 @@
     launch(streams[0])
     launch(streams[1])
     weights.start()
+    loads[-1].wait()
+    for i in range(rows):
+        gs[i] = (cot_ref[i].astype(jnp.float32) * hidden_t[:, i : i + 1]).astype(jnp.bfloat16)
     launch(streams[2])
 
     for row_src, col_src, dst, _, _ in streams:
@@ -660,8 +679,7 @@
     for w_ref, at, first in ((wa, mine, col_part[0]), (wb, rest, col_part[1])):
         acc = (first + back_project(grow, 0, w_ref)).reshape(rows, cols, part)
         for i in range(rows):
-            flags = flag_ref[i]
-            keep = flags[:, 1:2] * (1.0 - flags[:, 0:1])
+            keep = present_t[:, i : i + 1] * (1.0 - hidden_t[:, i : i + 1])
             pg_ref[i, :, pl.ds(at, part)] = (acc[i] * keep).astype(pg_ref.dtype)
 
     for q in order[:-1]:
@@ -709,10 +727,9 @@
     width = 2 * half + 2 * N
     slab = feat // (2 * chips)
     depth = chips // 2
-    flags = jnp.stack([masked, tissue], axis=2).astype(jnp.float32)
     bf, fl = jnp.bfloat16, jnp.float32
     vmem, dma = pltpu.VMEM, pltpu.SemaphoreType.DMA
-    in_vmem, anywhere = pl.BlockSpec(memory_space=pltpu.VMEM), pl.BlockSpec(memory_space=pl.ANY)
+    in_vmem, anywhere = pl.BlockSpec(memory_space=pltpu.VMEM), pl.BlockSpec(memory_space=pltpu.HBM)
     scale = 1.0 / math.sqrt(2 * rows * cols * chips)
     return pl.pallas_call(
         functools.partial(layer_kernel, chips, rows, scale),
@@ -721,9 +738,12 @@
             jax.ShapeDtypeStruct(patches.shape, bf),
             jax.ShapeDtypeStruct((slab, 2 * half), fl),
         ),
-        in_specs=[in_vmem] * 6 + [anywhere] * 2,
+        in_specs=[anywhere] * 9,
         out_specs=(in_vmem, in_vmem),
         scratch_shapes=[
+            vmem(patches.shape, bf), vmem(mask_token.shape, bf), vmem(patches.shape, bf),
+            vmem(masked.shape, masked.dtype), vmem(tissue.shape, tissue.dtype),
+            vmem(row_decay.shape, fl), vmem(col_decay.shape, fl), dma((7,)),
             vmem((rows, cols, feat), bf), vmem((rows, cols, feat), bf),
             vmem((rows, heads, cols), fl), vmem((rows, heads, cols), fl),
             vmem((chips, cols, feat), bf), vmem((chips, cols, feat), bf), vmem((chips, heads, cols), fl),
@@ -741,10 +761,10 @@
             dma((2 * depth,)), dma((2 * depth,)),
         ],
         compiler_params=pltpu.CompilerParams(
-            collective_id=0, has_side_effects=True, vmem_limit_bytes=48 << 20
+            collective_id=0, has_side_effects=True, vmem_limit_bytes=60 << 20
         ),
     )(
-        patches, mask_token.reshape(1, feat), cotangent, flags, row_decay, col_decay,
+        patches, mask_token, cotangent, masked, tissue, row_decay, col_decay,
         in_weight, out_weight,
     )
 

time: 50.1 us -> 42.8 us (0.85)
  the two profiles are of different devices: /device:TPU:27 before, /device:TPU:1 now
where the time goes in v1:
time: 42.8 us; the launch traced here: 42.6 us
  Pallas kernels  38.7 us (90%)
  local copies, waits for them, and re-layouts  3.34 us (8%)
  between operations  0.64 us (1%)
    pallas_call x1, Pallas kernels, owned(): pl.pallas_call(functools.partial(layer_kernel, chips, rows, scale), name=...  38.7 us
    unnamed x2, local copies, waits for them, and re-layouts  3.34 us

profile of v1, /device:TPU:1, one launch (start us, length us, event | category | flops | bytes accessed | tf_op | source)
XLA Modules:
  0.0 42.6 jit_solution(8402417233675584132)
XLA Ops:
  0.6 38.7 %layer.1 = (bf16[4,32,1024]{2,1,0:T(8,128)(2,1)}, f32[64,1024]{1,0:T(8,128)}) custom-call(bf16[4,32,1024]{2,1,0:T(8,128)(2,1)} %patch_hbm.1, bf16[1024]{0:T(1024)(128)(2,1)} %token_hbm.1, bf16[4,32,1024]{2,1,0:T(8,128)(2,1)} %cot_hbm.1, s32[4,32]{1,0:T(4,128)} %hidden_hbm.1, s32[4,32]{1,0:T(4,128)} %present_hbm.1, f32[8,4,32]{2,1,0:T(4,128)} %rdec_hbm.1, ...), custom_call_target="tpu_custom_call" | custom-call | tf_op jit(solution)/shard_map/layer/pallas_call | solution.py:734
  39.3 1.7 %copy.13 = bf16[4,32,1024]{2,1,0:T(8,128)(2,1)} copy(bf16[4,32,1024]{2,1,0:T(8,128)(2,1)} %get-tuple-element.4) | data formatting | bytes 524288
  41.0 1.7 %copy.14 = f32[64,1024]{1,0:T(8,128)} copy(f32[64,1024]{1,0:T(8,128)} %get-tuple-element.5) | data formatting | bytes 524288

commit v2 on v1

--- a/solution.py
+++ b/solution.py
@@ -577,6 +577,22 @@
         xsend[q] = weight_block(2 * q + 1 - xi).astype(jnp.bfloat16)
         across(q).start()
 
+    def along(q, core):
+        return remote(
+            zs.at[q, core], zr.at[zi, c], z_send.at[2 * q + core], z_recv.at[2 * zi + c], 2 * q + xi, core
+        )
+
+    def forward(q):
+        across(q).wait_recv()
+        both = wgo[q] + xr[q].astype(jnp.float32)
+        wgo[q] = both
+        zs[q] = both.astype(jnp.bfloat16).reshape(2, both.shape[0] // 2, both.shape[1])
+
+    def forward_far(q):
+        forward(q)
+        for core in range(2):
+            along(q, core).start()
+
     grads = gb[...].reshape(toks, feat)
     gn_s[...] = mm(grads, wout[...], NN).astype(jnp.bfloat16)
     d_scores = jnp.zeros((toks, toks), jnp.float32)
@@ -599,6 +615,10 @@
         zero = jnp.zeros_like(dy)
         d_scores += dec_s[2 * p] * mm(jnp.where(low, dy, zero).astype(jnp.bfloat16), val_bf, NT)
         d_scores += dec_s[2 * p + 1] * mm(jnp.where(low, zero, dy).astype(jnp.bfloat16), val_bf, NT)
+        if p < depth:
+            wgo[order[p]] = weight_block(2 * order[p] + xi)
+        if p == 2:
+            forward_far(order[0])
     ds_bf = d_scores.astype(jnp.bfloat16)
     d_bc = jnp.concatenate([mm(ds_bf, c_bf, TN), mm(ds_bf, b_bf, NN)], axis=1)
     gp[:, :, 2 * half :] = d_bc.astype(jnp.bfloat16).reshape(chips, cols, 2 * N)
@@ -631,25 +651,6 @@
     def _():
         col_back(0).start()
         gcol[...] = gp[pl.ds(rows, rows)]
-
-    for q in range(depth):
-        wgo[q] = weight_block(2 * q + xi)
-
-    def along(q, core):
-        return remote(
-            zs.at[q, core], zr.at[zi, c], z_send.at[2 * q + core], z_recv.at[2 * zi + c], 2 * q + xi, core
-        )
-
-    def forward(q):
-        across(q).wait_recv()
-        both = wgo[q] + xr[q].astype(jnp.float32)
-        wgo[q] = both
-        zs[q] = both.astype(jnp.bfloat16).reshape(2, both.shape[0] // 2, both.shape[1])
-
-    def forward_far(q):
-        forward(q)
-        for core in range(2):
-            along(q, core).start()
 
     def back_project(src, g, w_ref):
         flat = src[...].reshape(rows * cols, 2 * half + 2 * N)
@@ -658,14 +659,16 @@
         at = 4 * half + g * 2 * N
         return acc + mm(flat[:, 2 * half :], w_ref[at : at + 2 * N, :], NN)
 
-    forward_far(order[0])
+    for q in order[half // 128 :]:
+        wgo[q] = weight_block(2 * q + xi)
+    forward_far(order[1])
 
     @pl.when(c == 0)
     def _():
         col_back(1).wait_recv()
 
     col_part = [back_project(gcol, 1, w_ref) for w_ref in (wa, wb)]
-    for q in order[1:-1]:
+    for q in order[2:-1]:
         forward_far(q)
     forward(zi)
     along(zi, 1 - c).start()

time: 42.8 us -> 45.9 us (1.072)
  the two profiles are of different devices: /device:TPU:1 before, /device:TPU:29 now
where the time goes in v2:
time: 45.9 us; the launch traced here: 45.7 us
  Pallas kernels  41.8 us (91%)
  local copies, waits for them, and re-layouts  3.34 us (7%)
  between operations  0.64 us (1%)
    pallas_call x1, Pallas kernels, owned(): pl.pallas_call(functools.partial(layer_kernel, chips, rows, scale), name=...  41.8 us
    unnamed x2, local copies, waits for them, and re-layouts  3.34 us

profile of v2, /device:TPU:29, one launch (start us, length us, event | category | flops | bytes accessed | tf_op | source)
XLA Modules:
  0.0 45.7 jit_solution(5581656322095575156)
XLA Ops:
  0.6 41.8 %layer.1 = (bf16[4,32,1024]{2,1,0:T(8,128)(2,1)}, f32[64,1024]{1,0:T(8,128)}) custom-call(bf16[4,32,1024]{2,1,0:T(8,128)(2,1)} %patch_hbm.1, bf16[1024]{0:T(1024)(128)(2,1)} %token_hbm.1, bf16[4,32,1024]{2,1,0:T(8,128)(2,1)} %cot_hbm.1, s32[4,32]{1,0:T(4,128)} %hidden_hbm.1, s32[4,32]{1,0:T(4,128)} %present_hbm.1, f32[8,4,32]{2,1,0:T(4,128)} %rdec_hbm.1, ...), custom_call_target="tpu_custom_call" | custom-call | tf_op jit(solution)/shard_map/layer/pallas_call | solution.py:737
  42.4 1.7 %copy.13 = bf16[4,32,1024]{2,1,0:T(8,128)(2,1)} copy(bf16[4,32,1024]{2,1,0:T(8,128)(2,1)} %get-tuple-element.4) | data formatting | bytes 524288
  44.1 1.7 %copy.14 = f32[64,1024]{1,0:T(8,128)} copy(f32[64,1024]{1,0:T(8,128)} %get-tuple-element.5) | data formatting | bytes 524288

commit v3 on v1

--- a/solution.py
+++ b/solution.py
@@ -572,7 +572,8 @@
     def across(q):
         return remote(xsend.at[q], xr.at[q], xr_send.at[q], xr_recv.at[q], 2 * zi + 1 - xi, c)
 
-    order = [lax.rem(zi + 1 + j, depth) for j in range(depth)]
+    far = sorted(range(1, depth), key=lambda j: -min(j, depth - j)) + [0]
+    order = [lax.rem(zi + j, depth) for j in far]
     for q in order:
         xsend[q] = weight_block(2 * q + 1 - xi).astype(jnp.bfloat16)
         across(q).start()
@@ -614,7 +615,7 @@
 
     @pl.when(c == 0)
     def _():
-        for d in range(1, chips):
+        for d in sorted(range(1, chips), key=lambda j: -min(j, chips - j)):
             row_back(lax.rem(k + d, chips)).start()
 
         @pl.when(home == 1)

time: 42.8 us -> 42.8 us (level)
  no operation moved by 1% of the time
where the time goes in v3:
time: 42.8 us; the launch traced here: 42.6 us
  Pallas kernels  38.7 us (90%)
  local copies, waits for them, and re-layouts  3.34 us (8%)
  between operations  0.64 us (1%)
    pallas_call x1, Pallas kernels, owned(): pl.pallas_call(functools.partial(layer_kernel, chips, rows, scale), name=...  38.7 us
    unnamed x2, local copies, waits for them, and re-layouts  3.34 us

profile of v3, /device:TPU:1, one launch (start us, length us, event | category | flops | bytes accessed | tf_op | source)
XLA Modules:
  0.0 42.6 jit_solution(1081354982369131780)
XLA Ops:
  0.6 38.7 %layer.1 = (bf16[4,32,1024]{2,1,0:T(8,128)(2,1)}, f32[64,1024]{1,0:T(8,128)}) custom-call(bf16[4,32,1024]{2,1,0:T(8,128)(2,1)} %patch_hbm.1, bf16[1024]{0:T(1024)(128)(2,1)} %token_hbm.1, bf16[4,32,1024]{2,1,0:T(8,128)(2,1)} %cot_hbm.1, s32[4,32]{1,0:T(4,128)} %hidden_hbm.1, s32[4,32]{1,0:T(4,128)} %present_hbm.1, f32[8,4,32]{2,1,0:T(4,128)} %rdec_hbm.1, ...), custom_call_target="tpu_custom_call" | custom-call | tf_op jit(solution)/shard_map/layer/pallas_call | solution.py:735
  39.3 1.7 %copy.13 = bf16[4,32,1024]{2,1,0:T(8,128)(2,1)} copy(bf16[4,32,1024]{2,1,0:T(8,128)(2,1)} %get-tuple-element.4) | data formatting | bytes 524288
  41.0 1.7 %copy.14 = f32[64,1024]{1,0:T(8,128)} copy(f32[64,1024]{1,0:T(8,128)} %get-tuple-element.5) | data formatting | bytes 524288
